TPU v7x, 32 devices: a whole 2x2x4 slice. The times are simulated.
32 devices in a mesh: wide: 8 (over y, x, core), narrow: 4 (over z).
Axes of the slice: x: 2, y: 2, z: 4, core: 2. Of those that a mesh axis runs over, the one named last changes fastest.
Arguments:
- cache: bfloat16 [8, 8192, 128], P('wide', 'narrow'), may hold values from -6 to 6
- lookup_slots: int32 [8, 4096, 16], P('wide'), may hold values from 0 to 8191
- bag_lengths: int32 [8, 4096], P('wide'), may hold values from 1 to 16
- miss_rows: bfloat16 [8, 4096, 128], P('wide', 'narrow'), may hold values from -6 to 6
- miss_slots: int32 [8, 4096], P('wide', 'narrow'), may hold values from 0 to 8191, as said below
- holder_counts: int32 [8, 16], P('wide', 'narrow'), may hold values from 0 to 512, as said below
- w_first: bfloat16 [1024, 4096], P(None, 'narrow'), may hold values from -0.1875 to 0.1875
- b_first: float32 [4096], P('narrow'), may hold values from -4 to 4
- w_second: bfloat16 [4096, 4096], P('narrow'), may hold values from -0.09375 to 0.09375
- b_second: float32 [4096], P('narrow'), may hold values from -4 to 4
- w_out: bfloat16 [4096], P('narrow'), may hold values from -0.09375 to 0.09375
Outputs:
- top_hidden: bfloat16 [4096, 4096], P('wide', 'narrow')
- logits: float32 [4096], P('wide')
- cache_next: bfloat16 [8, 8192, 128], P('wide', 'narrow')
Inputs may be any that keep to these rules, and one draw needn't show every extreme that they name: `holder_counts`: entry h * 4 + o is the number of row blocks that holder h sections for owner o, the device holding slots o * 2048 to (o + 1) * 2048 - 1; a holder's counts sum to at most 1024, and this is reached by some holder of every table; the largest count, 512, is reached in every table. `miss_slots`: A holder's live entries are packed by owner, owner 0 first, as its counts say; each live entry names a slot of its owner, no slot twice in a table; entries past a holder's live ones are 0 and unused.
All inputs are finite; a program needn't handle non-finite values.
Results may differ from a plain program's by a relative error of at most 0.0076.
Values may be sent and summed in bfloat16 or wider, within the bound.
No kernel may reach another device: no remote copies, remote signals or barrier semaphores. Data moves between devices by JAX's collectives and lax.ppermute only.
A program may use at most 128 MiB of HBM per device.

v0:
```python
import math
import jax
import jax.numpy as jnp
from jax import lax
from jax.sharding import PartitionSpec as P

SEND_CAP = 512


def pool_rows(cache_table, lookups, lengths, owner_index):
    slot_count = cache_table.shape[0]
    emb_width = cache_table.shape[1]
    batch_rows, bag_size = lookups.shape
    local_slots = lookups - owner_index * slot_count
    usable = jnp.arange(bag_size, dtype=jnp.int32)[None, :] < lengths[:, None]
    usable = usable & (local_slots >= 0) & (local_slots < slot_count)
    safe_slots = jnp.clip(local_slots, 0, slot_count - 1)
    block_rows = math.gcd(batch_rows, 2048)
    block_count = batch_rows // block_rows

    def pool_block(member):
        positions, keep = member
        gathered = jnp.take(cache_table, positions, axis=0).astype(jnp.float32)
        return jnp.sum(jnp.where(keep[..., None], gathered, jnp.zeros((), jnp.float32)), axis=1)

    pooled = lax.map(
        pool_block,
        (
            safe_slots.reshape(block_count, block_rows, bag_size),
            usable.reshape(block_count, block_rows, bag_size),
        ),
    )
    return pooled.reshape(batch_rows, emb_width)


def body(
    cache,
    lookup_slots,
    bag_lengths,
    miss_rows,
    miss_slots,
    holder_counts,
    w_first,
    b_first,
    w_second,
    b_second,
    w_out,
):
    wide_count = lax.axis_size("wide")
    narrow_count = lax.axis_size("narrow")
    owner_index = lax.axis_index("narrow")
    cache_table = cache[0]
    slot_count = cache_table.shape[0]
    emb_width = cache_table.shape[1]
    lookups = lookup_slots[0]
    lengths = bag_lengths[0]
    batch_rows, bag_size = lookups.shape
    owner_rows = batch_rows // wide_count
    quarter_rows = owner_rows // narrow_count
    whole_table = lax.all_gather(cache_table, "narrow", axis=0, tiled=True)
    own_lookups = lax.dynamic_index_in_dim(
        lookups.reshape(wide_count, narrow_count, quarter_rows, bag_size),
        owner_index,
        1,
        keepdims=False,
    )
    own_lengths = lax.dynamic_index_in_dim(
        lengths.reshape(wide_count, narrow_count, quarter_rows), owner_index, 1, keepdims=False
    )
    own_pooled = pool_rows(
        whole_table,
        own_lookups.reshape(wide_count * quarter_rows, bag_size),
        own_lengths.reshape(wide_count * quarter_rows),
        0,
    )
    summed = own_pooled.reshape(1, wide_count, quarter_rows, emb_width).astype(jnp.bfloat16)
    arrived = lax.all_to_all(summed, "wide", split_axis=1, concat_axis=0, tiled=True)
    arrived = arrived.reshape(wide_count, quarter_rows, emb_width)
    pooled = lax.all_gather(arrived, "narrow", axis=1, tiled=True)
    first_slab = w_first.reshape(wide_count, emb_width, w_first.shape[1])
    first_terms = jnp.einsum("fbe,feh->bh", pooled, first_slab, preferred_element_type=jnp.float32)
    first_hidden = jnp.maximum(first_terms + b_first, 0.0).astype(jnp.bfloat16)
    second_terms = jnp.dot(first_hidden, w_second, preferred_element_type=jnp.float32)
    second_summed = lax.psum_scatter(second_terms, "narrow", scatter_dimension=1, tiled=True)
    top_hidden = jnp.maximum(second_summed + b_second, 0.0).astype(jnp.bfloat16)
    logit_terms = jnp.dot(top_hidden, w_out, preferred_element_type=jnp.float32)
    logits = lax.psum(logit_terms, "narrow")
    sectioned = miss_rows[0]
    sectioned_slots = miss_slots[0]
    sectioned_counts = holder_counts[0]
    hold_rows = sectioned.shape[0]
    send_cap = SEND_CAP
    starts = jnp.cumsum(sectioned_counts) - sectioned_counts
    column_ids = jnp.arange(send_cap, dtype=jnp.int32)
    live = column_ids[None, :] < sectioned_counts[:, None]
    sources = jnp.where(live, starts[:, None] + column_ids[None, :], -1).reshape(
        narrow_count * send_cap
    )
    selector = (sources[:, None] == jnp.arange(hold_rows, dtype=jnp.int32)[None, :]).astype(
        jnp.bfloat16
    )
    slab_rows = jnp.dot(selector, sectioned, preferred_element_type=jnp.float32).astype(
        jnp.bfloat16
    )
    slab_rows = slab_rows.reshape(narrow_count, send_cap, emb_width)
    slab_slots = jnp.where(
        sources >= 0, jnp.take(sectioned_slots, jnp.maximum(sources, 0), axis=0), -1
    )
    slab_slots = slab_slots.reshape(narrow_count, send_cap)
    got_rows, got_slots = (
        lax.all_to_all(slab_rows, "narrow", split_axis=0, concat_axis=0, tiled=True),
        lax.all_to_all(slab_slots, "narrow", split_axis=0, concat_axis=0, tiled=True),
    )
    arrived_rows = got_rows.reshape(narrow_count * send_cap, emb_width)
    arrived_slots = got_slots.reshape(narrow_count * send_cap)
    targets = arrived_slots - owner_index * slot_count
    kept = (arrived_slots >= 0) & (targets >= 0) & (targets < slot_count)
    targets = jnp.where(kept, targets, -1)
    placing = (targets[:, None] == jnp.arange(slot_count, dtype=jnp.int32)[None, :]).astype(
        jnp.bfloat16
    )
    placed = jnp.einsum("as,ae->se", placing, arrived_rows, preferred_element_type=jnp.float32)
    struck = jnp.sum(placing.astype(jnp.float32), axis=0) > 0.5
    cache_next = jnp.where(struck[:, None], placed.astype(jnp.bfloat16), cache_table)[None]
    return (top_hidden, logits, cache_next)


def solution(mesh):
    return jax.shard_map(
        body,
        mesh=mesh,
        in_specs=(
            P("wide", "narrow", None),
            P("wide", None, None),
            P("wide", None),
            P("wide", "narrow", None),
            P("wide", "narrow"),
            P("wide", "narrow"),
            P(None, "narrow"),
            P("narrow"),
            P("narrow", None),
            P("narrow"),
            P("narrow"),
        ),
        out_specs=(P("wide", "narrow"), P("wide"), P("wide", "narrow", None)),
        check_vma=False,
    )
```

profile of v0, /device:TPU:0, one launch (start us, length us, event | category | flops | bytes accessed | tf_op | source)
XLA Modules:
  0.0 345.0 jit_solution(8075441370404629953)
XLA Ops:
  7.2 0.7 all-gather.5.cloned.1.call-update
  8.0 1.1 reshape_squeeze.7
  9.1 0.7 constant_dynamic-slice_fusion.1
  10.0 0.3 copy.29
  11.0 46.9 %all-gather.5.cloned.1.call-done = bf16[1,8192,128]{2,1,0:T(8,128)(2,1)} async-done(((bf16[1,2048,128]{2,1,0:T(8,128)(2,1)}), bf16[1,8192,128]{2,1,0:T(8,128)(2,1)}) %all-gather.5.cloned.1.call-update) | async-done | bytes 2097168 | tf_op jit(solution)/shard_map/all_gather | solution.py:60
  58.0 57.2 %gather_fusion = bf16[16384,128]{1,0:T(8,128)(2,1)} fusion(bf16[8192,128]{1,0:T(8,128)(2,1)} %bitcast.81, s32[16384]{0:T(1024)S(1)} %broadcast_clamp_fusion), kind=kCustom, calls=%fused_computation | custom fusion | bytes 8454144 | tf_op jit(solution)/shard_map/while/body/eval_jaxpr/jit(_take)/gather | solution.py:23
  115.2 7.3 %select_reduce_fusion = bf16[1024,128]{1,0:T(8,128)(2,1)S(1)} fusion(pred[1024,16]{1,0:T(8,128)(4,1)S(1)} %copy.30, pred[1024,16]{1,0:T(8,128)(4,1)S(1)} %copy.29, bf16[16384,128]{1,0:T(8,128)(2,1)} %gather_fusion), kind=kLoop, calls=%fused_computation.8 | loop fusion | flops 8257536 | bytes 4489216 | tf_op jit(solution)/shard_map/while/body/eval_jaxpr/reduce_sum | solution.py:24
  122.5 10.5 %all_to_all.20 = bf16[1,8,128,128]{3,2,0,1:T(8,128)(2,1)} all-to-all(bf16[1,8,128,128]{3,2,0,1:T(8,128)(2,1)S(1)} %bitcast.82), channel_id=1, replica_groups=mesh['wide'=8,'narrow'=4] {'wide'}, dimensions={1} | all-to-all | bytes 524288 | tf_op jit(solution)/shard_map/all_to_all | solution.py:77
  133.1 25.1 %all-gather.7.cloned.1.call-done = bf16[1,8,512,128]{3,2,1,0:T(8,128)(2,1)} async-done(((bf16[1,8,128,128]{3,2,1,0:T(8,128)(2,1)}), bf16[1,8,512,128]{3,2,1,0:T(8,128)(2,1)}) %all-gather.7.cloned.1.call-update) | async-done | bytes 1048592 | tf_op jit(solution)/shard_map/all_gather | solution.py:79
  158.1 12.5 %fusion.13 = f32[512,4096]{1,0:T(8,128)} fusion(bf16[1024,4096]{1,0:T(8,128)(2,1)} %param.19, bf16[8,128,1024]{2,1,0:T(8,128)(2,1)S(1)} %bitcast.79, bf16[1,8,512,128]{3,2,1,0:T(8,128)(2,1)} %all-gather.7.cloned.1.call-done, f32[1024]{0:T(1024)S(1)} %copy-done.8), kind=kOutput, calls=%fused_computation.21 | convolution fusion | flops 5370281984 | bytes 19927040 | tf_op jit(solution)/shard_map/dot_general | solution.py:83
  170.7 0.6 copy-done.6
  171.6 8.6 %gather_fusion.1 = s32[2048]{0:T(1024)S(1)} fusion(s32[1024]{0:T(1024)S(1)} %bitcast.80, s32[2048]{0:T(1024)S(1)} %broadcast_clamp_fusion.2), kind=kCustom, calls=%fused_computation.1 | custom fusion | bytes 24576 | tf_op jit(solution)/shard_map/jit(_take)/gather | solution.py:107
  180.2 0.7 compare_select_fusion.3
  180.9 3.2 all-to-all-start.1
  184.2 2.4 fusion.5
  186.6 3.3 all-to-all-done.1
  189.9 3.7 %all-to-all-start.2 = ((bf16[4,512,128]{2,1,0:T(8,128)(2,1)}), bf16[4,512,128]{2,1,0:T(8,128)(2,1)S(1)}, u32[]{:S(2)}, u32[]{:S(2)}) async-start(bf16[4,512,128]{2,1,0:T(8,128)(2,1)} %bitcast.18), calls=%async_computation.3 | async-start | bytes 1048576 | tf_op jit(solution)/shard_map/all_to_all | solution.py:111
  193.7 2.1 convert_reduce_fusion
  195.7 26.5 %all-to-all-done.2 = bf16[4,512,128]{2,1,0:T(8,128)(2,1)S(1)} async-done(((bf16[4,512,128]{2,1,0:T(8,128)(2,1)}), bf16[4,512,128]{2,1,0:T(8,128)(2,1)S(1)}, u32[]{:S(2)}, u32[]{:S(2)}) %all-to-all-start.2) | async-done | bytes 524320 | tf_op jit(solution)/shard_map/all_to_all | solution.py:111
  222.2 5.8 %fusion.8 = bf16[1,2048,128]{2,1,0:T(8,128)(2,1)} fusion(bf16[2048,128]{1,0:T(8,128)(2,1)S(1)} %bitcast.87, s32[2048]{0:T(1024)S(1)} %and_select_fusion, bf16[1,2048,128]{2,1,0:T(8,128)(2,1)S(1)} %copy-done.3, pred[2048]{0:T(1024)(128)(4,1)S(1)} %broadcast_compare_fusion.2), kind=kOutput, calls=%fused_computation.14 | convolution fusion | flops 1078460416 | bytes 1583104 | tf_op jit(solution)/shard_map/as,ae->se/dot_general | solution.py:122
  228.0 95.3 %reduce-scatter.2.cloned.1.call-done = f32[512,1024]{1,0:T(8,128)} async-done(((f32[512,4096]{1,0:T(8,128)}), f32[512,1024]{1,0:T(8,128)}) %reduce-scatter.2.cloned.1.call-update) | async-done | bytes 2097168 | tf_op jit(solution)/shard_map/reduce_scatter | solution.py:84
  323.3 1.9 maximum_convert_fusion
  325.2 0.4 fusion.20
  325.6 12.9 %psum.7 = f32[512]{0:T(512)} all-reduce(f32[512]{0:T(512)S(1)} %bitcast.94), channel_id=1, replica_groups=mesh['wide'=8,'narrow'=4] {'narrow'}, use_global_device_ids=true, to_apply=%region_2.3 | all-reduce | flops 512 | bytes 4096 | tf_op jit(solution)/shard_map/psum | solution.py:87
  (44 shorter events, 1.4 us)
Async XLA Ops:
  7.2 151.0 %copy-start = (bf16[1024,1024]{1,0:T(8,128)(2,1)S(1)}, bf16[1024,1024]{1,0:T(8,128)(2,1)}, u32[]{:S(2)}) copy-start(bf16[1024,1024]{1,0:T(8,128)(2,1)} %param.17) | copy-start | bytes 6291460
  7.2 50.8 %all-gather.5.cloned.1.call-start = ((), (), s32[]{:S(2)}) async-start(), calls=%async_computation.5 | async-start | bytes 2621440 | tf_op jit(solution)/shard_map/all_gather | solution.py:60
  7.9 150.2 %all-gather.7.cloned.1.call-start = ((), (), s32[]{:S(2)}) async-start(), calls=%async_computation.6 | async-start | bytes 1310720 | tf_op jit(solution)/shard_map/all_gather | solution.py:79
  115.2 42.9 %copy-start.8 = (f32[1024]{0:T(1024)S(1)}, f32[1024]{0:T(1024)}, u32[]{:S(2)}) copy-start(f32[1024]{0:T(1024)} %param.18) | copy-start | bytes 12292
  133.0 190.3 %reduce-scatter.2.cloned.1.call-start = ((), (), s32[]{:S(2)}) async-start(), calls=%async_computation.4 | async-start | bytes 10485760 | tf_op jit(solution)/shard_map/reduce_scatter | solution.py:84
  170.7 0.7 copy-start.6
  170.7 0.9 copy-start.1
  171.6 12.6 %copy-start.7 = (bf16[1,1024,128]{2,1,0:T(8,128)(2,1)S(1)}, bf16[1,1024,128]{2,1,0:T(8,128)(2,1)}, u32[]{:S(2)}) copy-start(bf16[1,1024,128]{2,1,0:T(8,128)(2,1)} %param.14) | copy-start | bytes 786436
  180.2 6.4 %copy-start.5 = (bf16[1024]{0:T(1024)(128)(2,1)S(1)}, bf16[1024]{0:T(1024)(128)(2,1)}, u32[]{:S(2)}) copy-start(bf16[1024]{0:T(1024)(128)(2,1)} %param.21) | copy-start | bytes 6148
  180.2 42.0 %copy-start.3 = (bf16[1,2048,128]{2,1,0:T(8,128)(2,1)S(1)}, bf16[1,2048,128]{2,1,0:T(8,128)(2,1)}, u32[]{:S(2)}) copy-start(bf16[1,2048,128]{2,1,0:T(8,128)(2,1)} %param.11) | copy-start | bytes 1572868
  180.9 9.0 %all-to-all-start.1 = ((s32[4,1,512]{2,1,0:T(1,128)}), s32[4,1,512]{2,1,0:T(1,128)S(1)}, u32[]{:S(2)}, u32[]{:S(2)}) async-start(s32[4,1,512]{2,1,0:T(1,128)} %compare_select_fusion.3), calls=%async_computation.2 | async-start | bytes 16384 | tf_op jit(solution)/shard_map/all_to_all | solution.py:112
  189.9 32.3 %all-to-all-start.2 = ((bf16[4,512,128]{2,1,0:T(8,128)(2,1)}), bf16[4,512,128]{2,1,0:T(8,128)(2,1)S(1)}, u32[]{:S(2)}, u32[]{:S(2)}) async-start(bf16[4,512,128]{2,1,0:T(8,128)(2,1)} %bitcast.18), calls=%async_computation.3 | async-start | bytes 1048576 | tf_op jit(solution)/shard_map/all_to_all | solution.py:111
  222.2 101.1 %copy-start.4 = (f32[1024]{0:T(1024)S(1)}, f32[1024]{0:T(1024)}, u32[]{:S(2)}) copy-start(f32[1024]{0:T(1024)} %param.20) | copy-start | bytes 12292
  325.2 13.3 %copy-start.2 = (bf16[512,1024]{1,0:T(8,128)(2,1)}, bf16[512,1024]{1,0:T(8,128)(2,1)S(1)}, u32[]{:S(2)}) copy-start(bf16[512,1024]{1,0:T(8,128)(2,1)S(1)} %maximum_convert_fusion) | copy-start | bytes 3145732
Sparse Core Ops, SparseCore 0:
  9.6 48.3 all-gather.4
  133.1 24.9 all-gather.6
  170.8 152.4 reduce-scatter.1
where the time goes:
time: 346 us; the launch traced here: 345 us
  waiting for transfers between devices  198 us (57%)
  local copies, waits for them, and re-layouts  69.3 us (20%)
  blocking collectives  23.4 us (7%)
  matrix products  21.1 us (6%)
  between operations  14 us (4%)
  other arithmetic  12.4 us (4%)
  starting transfers between devices  7.02 us (2%)
    reduce_scatter x1, waiting for transfers between devices, body(): lax.psum_scatter(second_terms, 'narrow', scatter_dimension=1, tiled=True)  95.3 us
    gather x1, local copies, waits for them, and re-layouts, pool_block(): gathered = jnp.take(cache_table, positions, axis=0).astype(jnp.float32)  57.2 us
    all_gather x1, waiting for transfers between devices, body(): whole_table = lax.all_gather(cache_table, 'narrow', axis=0, tiled=True)  46.9 us
    all_to_all x1, waiting for transfers between devices, body(): lax.all_to_all(slab_rows, 'narrow', split_axis=0, concat_axis=0, tiled=True)  26.5 us
    all_gather x1, waiting for transfers between devices, body(): pooled = lax.all_gather(arrived, 'narrow', axis=1, tiled=True)  25.1 us
    psum x1, blocking collectives, body(): logits = lax.psum(logit_terms, 'narrow')  12.9 us
    dot_general x1, matrix products, body(): jnp.dot(first_hidden, w_second, preferred_element_type=jnp.float32)  12.5 us
    all_to_all x1, blocking collectives, body(): lax.all_to_all(summed, 'wide', split_axis=1, concat_axis=0, tiled=True)  10.5 us
  transfers between devices with their start and end apart: 5, of which 5 were waited for; matrix products, arithmetic and copies ran while one was open for 7% of the time, Pallas kernels for 0%

commit v1 on v0

--- a/solution.py
+++ b/solution.py
@@ -5,6 +5,31 @@
 from jax.sharding import PartitionSpec as P
 
 SEND_CAP = 512
+
+
+def laid_out(tiles, dim):
+    tiles = jnp.moveaxis(tiles, 0, dim)
+    shape = tiles.shape
+    return tiles.reshape(*shape[:dim], shape[dim] * shape[dim + 1], *shape[dim + 2 :])
+
+
+def ring_apply(x, axis, dim, apply, out_dim):
+    devices, index, rows = (lax.axis_size(axis), lax.axis_index(axis), x.shape[dim])
+    ahead = [(i, (i + 1) % devices) for i in range(devices)]
+    left = [(i, (i - 1) % devices) for i in range(devices)]
+    half = devices // 2
+    tiles = {}
+    from_left = from_right = x
+    for step in range(half + 1):
+        next_left = lax.ppermute(from_left, axis, ahead) if step < half else None
+        next_right = lax.ppermute(from_right, axis, left) if step < devices - half - 1 else None
+        tiles[-step] = apply(from_left, (index - step) % devices * rows)
+        if 0 < step < devices - half:
+            tiles[step] = apply(from_right, (index + step) % devices * rows)
+        from_left, from_right = (next_left, next_right)
+    tiles = jnp.stack([tiles[k] for k in sorted(tiles)])
+    tiles = tiles[(jnp.arange(devices) - index + half) % devices]
+    return laid_out(tiles, out_dim)
 
 
 def pool_rows(cache_table, lookups, lengths, owner_index):
@@ -76,9 +101,16 @@
     summed = own_pooled.reshape(1, wide_count, quarter_rows, emb_width).astype(jnp.bfloat16)
     arrived = lax.all_to_all(summed, "wide", split_axis=1, concat_axis=0, tiled=True)
     arrived = arrived.reshape(wide_count, quarter_rows, emb_width)
-    pooled = lax.all_gather(arrived, "narrow", axis=1, tiled=True)
     first_slab = w_first.reshape(wide_count, emb_width, w_first.shape[1])
-    first_terms = jnp.einsum("fbe,feh->bh", pooled, first_slab, preferred_element_type=jnp.float32)
+    first_terms = ring_apply(
+        arrived,
+        "narrow",
+        1,
+        lambda shard, offset: jnp.einsum(
+            "fbe,feh->bh", shard, first_slab, preferred_element_type=jnp.float32
+        ),
+        0,
+    )
     first_hidden = jnp.maximum(first_terms + b_first, 0.0).astype(jnp.bfloat16)
     second_terms = jnp.dot(first_hidden, w_second, preferred_element_type=jnp.float32)
     second_summed = lax.psum_scatter(second_terms, "narrow", scatter_dimension=1, tiled=True)

time: 346 us -> 345 us (level)
  blocking collectives: 23.4 us -> 12.9 us
  starting transfers between devices: 7.02 us -> 14.5 us
  waiting for transfers between devices: 198 us -> 193 us
  other arithmetic: 12.4 us -> 16.5 us
  local copies, waits for them, and re-layouts: 69.3 us -> 72.9 us
    all_gather x1 -> x0, waiting for transfers between devices: 25.1 us -> none  [body(): pooled = lax.all_gather(arrived, 'narrow', axis=1, tiled=True)]
    ppermute x0 -> x3, waiting for transfers between devices: none -> 15.4 us  [the longest x2 13.7 us: ring_apply(): next_left = lax.ppermute(from_left, axis, ahead) if step < half else None]
    all_to_all x1 -> x0, blocking collectives: 10.5 us -> none  [body(): lax.all_to_all(summed, 'wide', split_axis=1, concat_axis=0, tiled=True)]
    all_to_all x0 -> x1, waiting for transfers between devices: none -> 6.83 us  [body(): lax.all_to_all(summed, 'wide', split_axis=1, concat_axis=0, tiled=True)]
    ppermute x0 -> x3, starting transfers between devices: none -> 3.83 us  [the longest x1 3.64 us: ring_apply(): lax.ppermute(from_right, axis, left)]
    all_to_all x0 -> x1, starting transfers between devices: none -> 3.66 us  [body(): lax.all_to_all(summed, 'wide', split_axis=1, concat_axis=0, tiled=True)]
    gather x0 -> x1, local copies, waits for them, and re-layouts: none -> 3.59 us  [ring_apply(): tiles = tiles[(jnp.arange(devices) - index + half) % devices]]
  transfers between devices with their start and end apart: 5 -> 8, of which waited for: 5 -> 8; matrix products, arithmetic and copies ran while one was open for 7% -> 7% of each run, Pallas kernels for 0% -> 0%
where the time goes in v1:
time: 345 us; the launch traced here: 344 us
  waiting for transfers between devices  193 us (56%)
  local copies, waits for them, and re-layouts  72.9 us (21%)
  matrix products  20.5 us (6%)
  other arithmetic  16.5 us (5%)
  starting transfers between devices  14.5 us (4%)
  between operations  14.3 us (4%)
  blocking collectives  12.9 us (4%)
    reduce_scatter x1, waiting for transfers between devices, body(): lax.psum_scatter(second_terms, 'narrow', scatter_dimension=1, tiled=True)  94.8 us
    gather x1, local copies, waits for them, and re-layouts, pool_block(): gathered = jnp.take(cache_table, positions, axis=0).astype(jnp.float32)  57.2 us
    all_gather x1, waiting for transfers between devices, body(): whole_table = lax.all_gather(cache_table, 'narrow', axis=0, tiled=True)  47 us
    all_to_all x1, waiting for transfers between devices, body(): lax.all_to_all(slab_rows, 'narrow', split_axis=0, concat_axis=0, tiled=True)  24.5 us
    ppermute x2, waiting for transfers between devices, ring_apply(): next_left = lax.ppermute(from_left, axis, ahead) if step < half else None  13.7 us
    psum x1, blocking collectives, body(): logits = lax.psum(logit_terms, 'narrow')  12.9 us
    dot_general x1, matrix products, body(): jnp.dot(first_hidden, w_second, preferred_element_type=jnp.float32)  10.1 us
    gather x1, local copies, waits for them, and re-layouts, body(): jnp.take(sectioned_slots, jnp.maximum(sources, 0), axis=0)  8.58 us
  transfers between devices with their start and end apart: 8, of which 8 were waited for; matrix products, arithmetic and copies ran while one was open for 7% of the time, Pallas kernels for 0%

profile of v1, /device:TPU:0, one launch (start us, length us, event | category | flops | bytes accessed | tf_op | source)
XLA Modules:
  0.0 344.1 jit_solution(5003428674383776828)
XLA Ops:
  11.0 47.0 %all-gather.3.cloned.1.call-done = bf16[1,8192,128]{2,1,0:T(8,128)(2,1)} async-done(((bf16[1,2048,128]{2,1,0:T(8,128)(2,1)}), bf16[1,8192,128]{2,1,0:T(8,128)(2,1)}) %all-gather.3.cloned.1.call-update) | async-done | bytes 2097168 | tf_op jit(solution)/shard_map/all_gather | solution.py:85
  58.0 57.2 %gather_fusion = bf16[16384,128]{1,0:T(8,128)(2,1)} fusion(bf16[8192,128]{1,0:T(8,128)(2,1)} %bitcast.100, s32[16384]{0:T(1024)S(1)} %broadcast_clamp_fusion), kind=kCustom, calls=%fused_computation | custom fusion | bytes 8454144 | tf_op jit(solution)/shard_map/while/body/eval_jaxpr/jit(_take)/gather | solution.py:48
  115.2 8.0 %select_reduce_fusion = bf16[1024,128]{1,0:T(8,128)(2,1)} fusion(pred[1024,16]{1,0:T(8,128)(4,1)S(1)} %copy.29, pred[1024,16]{1,0:T(8,128)(4,1)S(1)} %copy.28, bf16[16384,128]{1,0:T(8,128)(2,1)} %gather_fusion), kind=kLoop, calls=%fused_computation.9 | loop fusion | flops 8257536 | bytes 4489216 | tf_op jit(solution)/shard_map/while/body/eval_jaxpr/reduce_sum | solution.py:49
  123.2 3.7 %all-to-all-start = ((bf16[1,8,128,128]{3,2,0,1:T(8,128)(2,1)}), bf16[1,8,128,128]{3,2,0,1:T(8,128)(2,1)S(1)}, u32[]{:S(2)}, u32[]{:S(2)}) async-start(bf16[1,8,128,128]{3,2,0,1:T(8,128)(2,1)} %bitcast.5), calls=%async_computation | async-start | bytes 524288 | tf_op jit(solution)/shard_map/all_to_all | solution.py:102
  126.9 6.8 %all-to-all-done = bf16[1,8,128,128]{3,2,0,1:T(8,128)(2,1)S(1)} async-done(((bf16[1,8,128,128]{3,2,0,1:T(8,128)(2,1)}), bf16[1,8,128,128]{3,2,0,1:T(8,128)(2,1)S(1)}, u32[]{:S(2)}, u32[]{:S(2)}) %all-to-all-start) | async-done | bytes 262176 | tf_op jit(solution)/shard_map/all_to_all | solution.py:102
  133.9 3.6 %collective-permute-start.2 = (bf16[8,128,128]{2,1,0:T(8,128)(2,1)S(1)}, bf16[8,128,128]{2,1,0:T(8,128)(2,1)S(1)}, u32[]{:S(2)}, u32[]{:S(2)}) collective-permute-start(bf16[8,128,128]{2,1,0:T(8,128)(2,1)S(1)} %bitcast.102), channel_id=1, source_target_pairs={{0,3},{1,0},{2,1},{3,2},{4,7},{5,4},{6,5},{7,6},{8,11},{9,8},{10,9... | collective-permute-start | bytes 786440 | tf_op jit(solution)/shard_map/ppermute | solution.py:25
  138.0 6.7 %collective-permute-done = bf16[8,128,128]{2,1,0:T(8,128)(2,1)S(1)} collective-permute-done((bf16[8,128,128]{2,1,0:T(8,128)(2,1)S(1)}, bf16[8,128,128]{2,1,0:T(8,128)(2,1)S(1)}, u32[]{:S(2)}, u32[]{:S(2)}) %collective-permute-start) | collective-permute-done | bytes 262176 | tf_op jit(solution)/shard_map/ppermute | solution.py:24
  145.2 1.7 collective-permute-done.2
  147.3 7.0 %collective-permute-done.1 = bf16[8,128,128]{2,1,0:T(8,128)(2,1)S(1)} collective-permute-done((bf16[8,128,128]{2,1,0:T(8,128)(2,1)S(1)}, bf16[8,128,128]{2,1,0:T(8,128)(2,1)S(1)}, u32[]{:S(2)}, u32[]{:S(2)}) %collective-permute-start.1) | collective-permute-done | bytes 262176 | tf_op jit(solution)/shard_map/ppermute | solution.py:24
  154.8 1.5 pad_maximum_fusion
  156.3 3.6 %gather_fusion.1 = f32[4,128,1024]{2,1,0:T(8,128)} fusion(f32[4,128,1024]{2,1,0:T(8,128)} %pad_maximum_fusion, s32[1024]{0:T(1024)S(1)} %pad_clamp_fusion), kind=kCustom, calls=%fused_computation.1 | custom fusion | bytes 4194320 | tf_op jit(solution)/shard_map/gather | solution.py:31
  159.9 1.9 fusion.10
  161.7 10.1 %fusion.18 = f32[512,4096]{1,0:T(8,128)} fusion(bf16[512,1024]{1,0:T(8,128)(2,1)S(1)} %fusion.10, bf16[1024,4096]{1,0:T(8,128)(2,1)} %param.19), kind=kOutput, calls=%fused_computation.59 | convolution fusion | flops 4294967296 | bytes 17825792 | tf_op jit(solution)/shard_map/dot_general | solution.py:115
  172.8 8.6 %gather_fusion.2 = s32[2048]{0:T(1024)S(1)} fusion(s32[1024]{0:T(1024)S(1)} %bitcast.99, s32[2048]{0:T(1024)S(1)} %broadcast_clamp_fusion.2), kind=kCustom, calls=%fused_computation.2 | custom fusion | bytes 24576 | tf_op jit(solution)/shard_map/jit(_take)/gather | solution.py:139
  182.1 3.3 all-to-all-start.1
  185.4 2.4 fusion.5
  187.8 3.4 all-to-all-done.1
  191.2 3.7 %all-to-all-start.2 = ((bf16[4,512,128]{2,1,0:T(8,128)(2,1)}), bf16[4,512,128]{2,1,0:T(8,128)(2,1)S(1)}, u32[]{:S(2)}, u32[]{:S(2)}) async-start(bf16[4,512,128]{2,1,0:T(8,128)(2,1)} %bitcast.26), calls=%async_computation.3 | async-start | bytes 1048576 | tf_op jit(solution)/shard_map/all_to_all | solution.py:143
  194.9 2.1 convert_reduce_fusion
  197.0 24.5 %all-to-all-done.2 = bf16[4,512,128]{2,1,0:T(8,128)(2,1)S(1)} async-done(((bf16[4,512,128]{2,1,0:T(8,128)(2,1)}), bf16[4,512,128]{2,1,0:T(8,128)(2,1)S(1)}, u32[]{:S(2)}, u32[]{:S(2)}) %all-to-all-start.2) | async-done | bytes 524320 | tf_op jit(solution)/shard_map/all_to_all | solution.py:143
  221.5 5.8 %fusion.8 = bf16[1,2048,128]{2,1,0:T(8,128)(2,1)} fusion(bf16[2048,128]{1,0:T(8,128)(2,1)S(1)} %bitcast.106, s32[2048]{0:T(1024)S(1)} %and_select_fusion, bf16[1,2048,128]{2,1,0:T(8,128)(2,1)S(1)} %copy-done.3, pred[2048]{0:T(1024)(128)(4,1)S(1)} %broadcast_compare_fusion.2), kind=kOutput, calls=%fused_computation.15 | convolution fusion | flops 1078460416 | bytes 1583104 | tf_op jit(solution)/shard_map/as,ae->se/dot_general | solution.py:154
  227.3 94.8 %reduce-scatter.2.cloned.1.call-done = f32[512,1024]{1,0:T(8,128)} async-done(((f32[512,4096]{1,0:T(8,128)}), f32[512,1024]{1,0:T(8,128)}) %reduce-scatter.2.cloned.1.call-update) | async-done | bytes 2097168 | tf_op jit(solution)/shard_map/reduce_scatter | solution.py:116
  322.1 1.9 maximum_convert_fusion
  324.3 12.9 %psum.7 = f32[512]{0:T(512)} all-reduce(f32[512]{0:T(512)S(1)} %bitcast.113), channel_id=1, replica_groups=mesh['wide'=8,'narrow'=4] {'narrow'}, use_global_device_ids=true, to_apply=%region_2.3 | all-reduce | flops 512 | bytes 4096 | tf_op jit(solution)/shard_map/psum | solution.py:119
  (57 shorter events, 7.8 us)
Async XLA Ops:
  7.2 130.4 %copy-start = (bf16[1024,1024]{1,0:T(8,128)(2,1)S(1)}, bf16[1024,1024]{1,0:T(8,128)(2,1)}, u32[]{:S(2)}) copy-start(bf16[1024,1024]{1,0:T(8,128)(2,1)} %param.17) | copy-start | bytes 6291460
  7.2 50.8 %all-gather.3.cloned.1.call-start = ((), (), s32[]{:S(2)}) async-start(), calls=%async_computation.5 | async-start | bytes 2621440 | tf_op jit(solution)/shard_map/all_gather | solution.py:85
  123.2 10.6 %all-to-all-start = ((bf16[1,8,128,128]{3,2,0,1:T(8,128)(2,1)}), bf16[1,8,128,128]{3,2,0,1:T(8,128)(2,1)S(1)}, u32[]{:S(2)}, u32[]{:S(2)}) async-start(bf16[1,8,128,128]{3,2,0,1:T(8,128)(2,1)} %bitcast.5), calls=%async_computation | async-start | bytes 524288 | tf_op jit(solution)/shard_map/all_to_all | solution.py:102
  126.9 195.2 %reduce-scatter.2.cloned.1.call-start = ((), (), s32[]{:S(2)}) async-start(), calls=%async_computation.4 | async-start | bytes 10485760 | tf_op jit(solution)/shard_map/reduce_scatter | solution.py:116
  133.8 11.0 %collective-permute-start = (bf16[8,128,128]{2,1,0:T(8,128)(2,1)S(1)}, bf16[8,128,128]{2,1,0:T(8,128)(2,1)S(1)}, u32[]{:S(2)}, u32[]{:S(2)}) collective-permute-start(bf16[8,128,128]{2,1,0:T(8,128)(2,1)S(1)} %bitcast.101), channel_id=1, source_target_pairs={{0,1},{1,2},{2,3},{3,0},{4,5},{5,6},{6,7},{7,4},{8,9},{9,10},{10,1... | collective-permute-start | bytes 786440 | tf_op jit(solution)/shard_map/ppermute | solution.py:24
  133.9 12.9 %collective-permute-start.2 = (bf16[8,128,128]{2,1,0:T(8,128)(2,1)S(1)}, bf16[8,128,128]{2,1,0:T(8,128)(2,1)S(1)}, u32[]{:S(2)}, u32[]{:S(2)}) collective-permute-start(bf16[8,128,128]{2,1,0:T(8,128)(2,1)S(1)} %bitcast.102), channel_id=1, source_target_pairs={{0,3},{1,0},{2,1},{3,2},{4,7},{5,4},{6,5},{7,6},{8,11},{9,8},{10,9... | collective-permute-start | bytes 786440 | tf_op jit(solution)/shard_map/ppermute | solution.py:25
  144.7 9.6 %collective-permute-start.1 = (bf16[8,128,128]{2,1,0:T(8,128)(2,1)S(1)}, bf16[8,128,128]{2,1,0:T(8,128)(2,1)S(1)}, u32[]{:S(2)}, u32[]{:S(2)}) collective-permute-start(bf16[8,128,128]{2,1,0:T(8,128)(2,1)S(1)} %collective-permute-done), channel_id=1, source_target_pairs={{0,1},{1,2},{2,3},{3,0},{4,5},{5,6},{6,7},{7,4},{8,9},{9,10},{10,1... | collective-permute-start | bytes 786440 | tf_op jit(solution)/shard_map/ppermute | solution.py:24
  156.3 3.6 %copy-start.4 = (f32[1024]{0:T(1024)S(1)}, f32[1024]{0:T(1024)}, u32[]{:S(2)}) copy-start(f32[1024]{0:T(1024)} %param.18) | copy-start | bytes 12292
  171.8 0.7 copy-start.7
  171.9 0.9 copy-start.1
  172.8 12.6 %copy-start.8 = (bf16[1,1024,128]{2,1,0:T(8,128)(2,1)S(1)}, bf16[1,1024,128]{2,1,0:T(8,128)(2,1)}, u32[]{:S(2)}) copy-start(bf16[1,1024,128]{2,1,0:T(8,128)(2,1)} %param.14) | copy-start | bytes 786436
  182.1 9.1 %all-to-all-start.1 = ((s32[4,1,512]{2,1,0:T(1,128)}), s32[4,1,512]{2,1,0:T(1,128)S(1)}, u32[]{:S(2)}, u32[]{:S(2)}) async-start(s32[4,1,512]{2,1,0:T(1,128)} %compare_select_fusion.3), calls=%async_computation.2 | async-start | bytes 16384 | tf_op jit(solution)/shard_map/all_to_all | solution.py:144
  185.4 2.4 copy-start.6
  185.4 36.1 %copy-start.3 = (bf16[1,2048,128]{2,1,0:T(8,128)(2,1)S(1)}, bf16[1,2048,128]{2,1,0:T(8,128)(2,1)}, u32[]{:S(2)}) copy-start(bf16[1,2048,128]{2,1,0:T(8,128)(2,1)} %param.11) | copy-start | bytes 1572868
  191.2 30.3 %all-to-all-start.2 = ((bf16[4,512,128]{2,1,0:T(8,128)(2,1)}), bf16[4,512,128]{2,1,0:T(8,128)(2,1)S(1)}, u32[]{:S(2)}, u32[]{:S(2)}) async-start(bf16[4,512,128]{2,1,0:T(8,128)(2,1)} %bitcast.26), calls=%async_computation.3 | async-start | bytes 1048576 | tf_op jit(solution)/shard_map/all_to_all | solution.py:143
  221.5 100.6 %copy-start.5 = (f32[1024]{0:T(1024)S(1)}, f32[1024]{0:T(1024)}, u32[]{:S(2)}) copy-start(f32[1024]{0:T(1024)} %param.20) | copy-start | bytes 12292
  323.9 13.3 %copy-start.2 = (bf16[512,1024]{1,0:T(8,128)(2,1)}, bf16[512,1024]{1,0:T(8,128)(2,1)S(1)}, u32[]{:S(2)}) copy-start(bf16[512,1024]{1,0:T(8,128)(2,1)S(1)} %maximum_convert_fusion) | copy-start | bytes 3145732
Sparse Core Ops, SparseCore 0:
  9.6 48.3 all-gather.2
  172.0 150.0 reduce-scatter.1
